TPU v7x, 128 devices: a whole 4x4x4 slice. The times are simulated.
128 devices in a mesh: bucket: 8 (over y, core), member: 16 (over z, x).
Axes of the slice: x: 4, y: 4, z: 4, core: 2. Of those that a mesh axis runs over, the one named last changes fastest.
Arguments:
- loader_rows: float32 [8192, 4096], P(('bucket', 'member')), may hold values from -12 to 12
- dest_bucket: int32 [8192], P(('bucket', 'member')), may hold values from 0 to 7, as said below
- dest_slot: int32 [8192], P(('bucket', 'member')), may hold values from 0 to 127, as said below
- noise: float32 [32768, 4096], P(('bucket', 'member')), may hold values from -12 to 12
Outputs:
- targets: float32 [32768, 4096], P(('bucket', 'member'))
Inputs may be any that keep to these rules, and one draw needn't show every extreme that they name: Loaded row r goes to bucket group dest_bucket[r] on the device of that group with the same member index as its loader device. No loader device sends more than 16 rows to one bucket group; on every member index one bucket group receives exactly 16 rows from every loader device, and every bucket group is so filled on some member index. `dest_slot`: rows that reach the same device have distinct slots.
All inputs are finite; a program needn't handle non-finite values.
Results may differ from a plain program's by a relative error of at most 0.012.
The roundings to bfloat16 on the way count: a program that leaves them out, or rounds other values in their place, can miss the bound.
Values may be sent and summed in bfloat16 or wider, within the bound.
A program may use at most 128 MiB of HBM per device.

v0:
```python
import math
import jax
import jax.numpy as jnp
from jax import lax
from jax.sharding import PartitionSpec as P

ROWS_DEV = 128
ITERS = 4


def tile_cost(panel, noise_rows, noise_norm, width):
    cross_term = lax.dot_general(
        panel, noise_rows, (((1,), (1,)), ((), ())), preferred_element_type=jnp.float32
    )
    panel_wide = panel.astype(jnp.float32)
    return (
        jnp.sum(panel_wide * panel_wide, axis=1)[:, None] + noise_norm[None, :] - 2.0 * cross_term
    ) / width


def body(loader_rows, dest_bucket, dest_slot, noise):
    groups = lax.axis_size("bucket")
    width = loader_rows.shape[1]
    noise_count = noise.shape[0]
    capacity = ROWS_DEV // groups
    epsilon = 0.64 / math.sqrt(width)
    rounded = loader_rows.astype(jnp.bfloat16)
    hits = (dest_bucket[:, None] == jnp.arange(groups, dtype=jnp.int32)[None, :]).astype(jnp.int32)
    ranks = jnp.sum((jnp.cumsum(hits, axis=0) - 1) * hits, axis=1)
    position = dest_bucket * capacity + ranks
    send_rows = jnp.zeros((groups * capacity, width), jnp.bfloat16).at[position].set(rounded)
    send_slots = jnp.full((groups * capacity,), ROWS_DEV, jnp.int32).at[position].set(dest_slot)
    got_rows, got_slots = (
        lax.all_to_all(send_rows, "bucket", split_axis=0, concat_axis=0, tiled=True),
        lax.all_to_all(send_slots, "bucket", split_axis=0, concat_axis=0, tiled=True),
    )
    data_rows = jnp.zeros((ROWS_DEV, width), jnp.bfloat16).at[got_slots].set(got_rows, mode="drop")
    live_rows = (
        jnp.zeros((ROWS_DEV,), jnp.bfloat16)
        .at[got_slots]
        .set(jnp.ones(got_slots.shape, jnp.bfloat16), mode="drop")
    )
    noise_rows = noise.astype(jnp.bfloat16)
    noise_wide = noise_rows.astype(jnp.float32)
    noise_norm = jnp.sum(noise_wide * noise_wide, axis=1)
    whole_rows, whole_live = (
        lax.all_gather(data_rows, "member", axis=0, tiled=True),
        lax.all_gather(live_rows, "member", axis=0, tiled=True),
    )
    cost_tile = tile_cost(whole_rows, noise_rows, noise_norm, width)
    alive_rows = whole_live > 0.5
    col_pot = jnp.zeros((noise_count,), jnp.float32)
    exponent = jnp.zeros(cost_tile.shape, jnp.float32)
    col_total = jnp.ones((noise_count,), jnp.float32)
    for sweep_index in range(ITERS):
        scores = (col_pot[None, :] - cost_tile) / epsilon
        local_peak = jnp.max(scores, axis=1)
        row_peak = lax.pmax(local_peak, "member")
        row_total = lax.psum(jnp.sum(jnp.exp(scores - row_peak[:, None]), axis=1), "member")
        row_pot = -epsilon * (row_peak + jnp.log(row_total))
        col_scores = (row_pot[:, None] - cost_tile) / epsilon
        col_peak = jnp.max(jnp.where(alive_rows[:, None], col_scores, -jnp.inf), axis=0)
        exponent = jnp.where(alive_rows[:, None], jnp.exp(col_scores - col_peak[None, :]), 0.0)
        col_total = jnp.sum(exponent, axis=0)
        col_pot = -epsilon * (col_peak + jnp.log(col_total))
    weights = (exponent / col_total[None, :]).astype(jnp.bfloat16)
    targets = lax.dot_general(
        weights, whole_rows, (((0,), (0,)), ((), ())), preferred_element_type=jnp.float32
    )
    return targets


def solution(mesh):
    return jax.shard_map(
        body,
        mesh=mesh,
        in_specs=(
            P(("bucket", "member"), None),
            P(("bucket", "member")),
            P(("bucket", "member")),
            P(("bucket", "member"), None),
        ),
        out_specs=P(("bucket", "member"), None),
        check_vma=False,
    )
```

profile of v0, /device:TPU:2, one launch (start us, length us, event | category | flops | bytes accessed | tf_op | source)
XLA Modules:
  0.0 500.6 jit_solution(14216818540153028822)
XLA Ops:
  6.5 0.7 fusion.20
  7.3 0.1 reduce_window_sum.11
  7.4 0.8 select_reduce_fusion.7
  8.2 0.7 compare_select_fusion.1
  8.9 0.9 scatter_custom_fusion
  9.8 0.7 all_to_all.16
  10.5 4.5 all-to-all-start
  14.9 3.1 scatter_custom_fusion.2
  18.0 2.2 all-to-all-done
  20.2 3.6 all-to-all-start.1
  23.8 0.0 all-gather.3.cloned.1.call-start
  23.8 0.6 broadcast.141
  24.4 0.7 reduce.3
  25.1 0.1 all_to_all.18
  25.2 14.4 %all-to-all-done.1 = bf16[8,16,4096]{2,1,0:T(8,128)(2,1)S(1)} async-done(((bf16[8,16,4096]{2,1,0:T(8,128)(2,1)}), bf16[8,16,4096]{2,1,0:T(8,128)(2,1)S(1)}, u32[]{:S(2)}, u32[]{:S(2)}) %all-to-all-start.1) | async-done | bytes 1048608 | tf_op jit(solution)/shard_map/all_to_all | solution.py:34
  39.6 3.0 scatter_custom_fusion.3
  42.7 0.0 all-gather.3.cloned.1.call-update
  42.7 2.6 multiply_reduce_fusion.1
  45.3 1.3 scatter_custom_fusion.1
  46.6 21.6 %all-gather = bf16[16,1,128]{2,1,0:T(2,128)(2,1)S(1)} all-gather(bf16[1,1,128]{2,1,0:T(2,128)(2,1)S(1)} %bitcast.16), channel_id=1, replica_groups=mesh['bucket'=8,'member'=16] {'member'}, dimensions={0}, use_global_device_ids=true | all-gather | bytes 4352 | tf_op jit(solution)/shard_map/all_gather | solution.py:48
  68.2 86.4 %all-gather.3.cloned.1.call-done = bf16[2048,4096]{1,0:T(8,128)(2,1)} async-done(((bf16[128,4096]{1,0:T(8,128)(2,1)}), bf16[2048,4096]{1,0:T(8,128)(2,1)}) %all-gather.3.cloned.1.call-update) | async-done | bytes 16777232 | tf_op jit(solution)/shard_map/all_gather | solution.py:47
  154.6 7.5 %multiply_reduce_fusion = f32[2048]{0:T(1024)S(1)} fusion(bf16[2048,4096]{1,0:T(8,128)(2,1)} %all-gather.3.cloned.1.call-done), kind=kLoop, calls=%fused_computation.4 | loop fusion | flops 25163776 | bytes 16785408 | tf_op jit(solution)/shard_map/reduce_sum | solution.py:17
  162.1 3.1 copy-done
  165.3 7.8 %fusion.2 = (f32[2048]{0:T(1024)S(1)}, f32[2048,256]{1,0:T(8,128)S(1)}) fusion(bf16[2048,4096]{1,0:T(8,128)(2,1)S(1)} %copy-done, f32[256,4096]{1,0:T(8,128)} %param.7, f32[256]{0:T(256)S(1)} %multiply_reduce_fusion.1, f32[2048]{0:T(1024)S(1)} %multiply_reduce_fusion), kind=kOutput, calls=%fused_computation.30 | convolution fusion | flops 4299683840 | bytes 23086080 | tf_op jit(solution)/shard_map/dot_general | solution.py:12
  173.1 36.8 %pmax.28 = f32[2048]{0:T(1024)S(1)} all-reduce(f32[2048]{0:T(1024)S(1)} %get-tuple-element.5), channel_id=1, replica_groups=mesh['bucket'=8,'member'=16] {'member'}, use_global_device_ids=true, to_apply=%region_9.10 | all-reduce | flops 2048 | bytes 16384 | tf_op jit(solution)/shard_map/pmax | solution.py:58
  209.9 0.8 exponential_reduce_fusion.3
  210.7 38.9 %psum.28 = f32[2048]{0:T(1024)S(1)} all-reduce(f32[2048]{0:T(1024)S(1)} %exponential_reduce_fusion.3), channel_id=1, replica_groups=mesh['bucket'=8,'member'=16] {'member'}, use_global_device_ids=true, to_apply=%region_11.12 | all-reduce | flops 2048 | bytes 16384 | tf_op jit(solution)/shard_map/psum | solution.py:59
  249.6 0.7 select_reduce_fusion.6
  250.3 0.7 select_reduce_fusion.5
  251.0 0.3 fusion.3
  251.4 36.0 %pmax.29 = f32[2048]{0:T(1024)S(1)} all-reduce(f32[2048]{0:T(1024)S(1)} %fusion.3), channel_id=1, replica_groups=mesh['bucket'=8,'member'=16] {'member'}, use_global_device_ids=true, to_apply=%region_15.16 | all-reduce | flops 2048 | bytes 16384 | tf_op jit(solution)/shard_map/pmax | solution.py:58
  287.4 0.8 exponential_reduce_fusion.2
  288.2 38.0 %psum.29 = f32[2048]{0:T(1024)S(1)} all-reduce(f32[2048]{0:T(1024)S(1)} %exponential_reduce_fusion.2), channel_id=1, replica_groups=mesh['bucket'=8,'member'=16] {'member'}, use_global_device_ids=true, to_apply=%region_17.18 | all-reduce | flops 2048 | bytes 16384 | tf_op jit(solution)/shard_map/psum | solution.py:59
  326.2 0.7 select_reduce_fusion.4
  326.9 0.7 select_reduce_fusion.3
  327.6 0.3 fusion.4
  328.0 36.0 %pmax.30 = f32[2048]{0:T(1024)S(1)} all-reduce(f32[2048]{0:T(1024)S(1)} %fusion.4), channel_id=1, replica_groups=mesh['bucket'=8,'member'=16] {'member'}, use_global_device_ids=true, to_apply=%region_21.22 | all-reduce | flops 2048 | bytes 16384 | tf_op jit(solution)/shard_map/pmax | solution.py:58
  364.0 0.8 exponential_reduce_fusion.1
  364.8 38.0 %psum.30 = f32[2048]{0:T(1024)S(1)} all-reduce(f32[2048]{0:T(1024)S(1)} %exponential_reduce_fusion.1), channel_id=1, replica_groups=mesh['bucket'=8,'member'=16] {'member'}, use_global_device_ids=true, to_apply=%region_23.24 | all-reduce | flops 2048 | bytes 16384 | tf_op jit(solution)/shard_map/psum | solution.py:59
  402.9 0.7 select_reduce_fusion.2
  403.6 0.7 select_reduce_fusion.1
  404.3 0.3 fusion.5
  404.7 36.0 %pmax.31 = f32[2048]{0:T(1024)S(1)} all-reduce(f32[2048]{0:T(1024)S(1)} %fusion.5), channel_id=1, replica_groups=mesh['bucket'=8,'member'=16] {'member'}, use_global_device_ids=true, to_apply=%region_27.28 | all-reduce | flops 2048 | bytes 16384 | tf_op jit(solution)/shard_map/pmax | solution.py:58
  440.7 0.8 exponential_reduce_fusion
  441.5 38.2 %psum.31 = f32[2048]{0:T(1024)S(1)} all-reduce(f32[2048]{0:T(1024)S(1)} %exponential_reduce_fusion), channel_id=1, replica_groups=mesh['bucket'=8,'member'=16] {'member'}, use_global_device_ids=true, to_apply=%region_29.30 | all-reduce | flops 2048 | bytes 16384 | tf_op jit(solution)/shard_map/psum | solution.py:59
  479.7 0.7 select_reduce_fusion
  480.5 0.7 fusion.6
  481.2 12.6 %fusion.7 = f32[256,4096]{1,0:T(8,128)} fusion(bf16[2048,4096]{1,0:T(8,128)(2,1)} %all-gather.3.cloned.1.call-done, f32[2048,256]{1,0:T(8,128)S(1)} %get-tuple-element.6, f32[256]{0:T(256)S(1)} %fusion.6, f32[256]{0:T(256)S(1)} %select_reduce_fusion, f32[2048]{0:T(1024)S(1)} %add_multiply_fusion, pred[2048]{0:T(1024)(128)(4,1)S(1)} %compare_bitcast_fusion), kind=kOutput, calls=%fused_computation.35 | convolution fusion | flops 4298113024 | bytes 23080960 | tf_op jit(solution)/shard_map/dot_general | solution.py:67
  (11 shorter events, 0.1 us)
Async XLA Ops:
  10.5 9.7 %all-to-all-start = ((s32[8,16,1]{1,2,0:T(1,128)}), s32[8,16,1]{1,2,0:T(1,128)S(1)}, u32[]{:S(2)}, u32[]{:S(2)}) async-start(s32[8,16,1]{1,2,0:T(1,128)} %bitcast), calls=%async_computation | async-start | bytes 8192 | tf_op jit(solution)/shard_map/all_to_all | solution.py:35
  20.2 19.5 %all-to-all-start.1 = ((bf16[8,16,4096]{2,1,0:T(8,128)(2,1)}), bf16[8,16,4096]{2,1,0:T(8,128)(2,1)S(1)}, u32[]{:S(2)}, u32[]{:S(2)}) async-start(bf16[8,16,4096]{2,1,0:T(8,128)(2,1)} %bitcast.4), calls=%async_computation.1 | async-start | bytes 2097152 | tf_op jit(solution)/shard_map/all_to_all | solution.py:34
  23.8 130.8 %all-gather.3.cloned.1.call-start = ((), (), s32[]{:S(2)}) async-start(), calls=%async_computation.2 | async-start | bytes 17825792 | tf_op jit(solution)/shard_map/all_gather | solution.py:47
  154.6 10.7 %copy-start = (bf16[2048,4096]{1,0:T(8,128)(2,1)S(1)}, bf16[2048,4096]{1,0:T(8,128)(2,1)}, u32[]{:S(2)}) copy-start(bf16[2048,4096]{1,0:T(8,128)(2,1)} %all-gather.3.cloned.1.call-done) | copy-start | bytes 50331652
Sparse Core Ops, SparseCore 0:
  42.8 111.7 all-gather.2
where the time goes:
time: 501 us
  blocking collectives  319 us (64%)
  waiting for transfers between devices  103 us (21%)
  other arithmetic  26.2 us (5%)
  matrix products  20.4 us (4%)
  between operations  13.7 us (3%)
  local copies, waits for them, and re-layouts  9.75 us (2%)
  starting transfers between devices  8.07 us (2%)
    psum x4, blocking collectives, body(): lax.psum(jnp.sum(jnp.exp(scores - row_peak[:, None]), axis=1), 'member')  153 us
    pmax x4, blocking collectives, body(): row_peak = lax.pmax(local_peak, 'member')  145 us
    all_gather x1, waiting for transfers between devices, body(): lax.all_gather(data_rows, 'member', axis=0, tiled=True)  86.4 us
    all_gather x1, blocking collectives, body(): lax.all_gather(live_rows, 'member', axis=0, tiled=True)  21.6 us
    all_to_all x1, waiting for transfers between devices, body(): lax.all_to_all(send_rows, 'bucket', split_axis=0, concat_axis=0, tiled=True)  14.4 us
    dot_general x1, matrix products, body(): lax.dot_general(weights, whole_rows, (((0,), (0,)), ((), ())), preferred_...  12.6 us
  transfers between devices with their start and end apart: 3, of which 3 were waited for; matrix products, arithmetic and copies ran while one was open for 2% of the time, Pallas kernels for 0%

commit v1 on v0

--- a/solution.py
+++ b/solution.py
@@ -44,7 +44,9 @@
     noise_wide = noise_rows.astype(jnp.float32)
     noise_norm = jnp.sum(noise_wide * noise_wide, axis=1)
     whole_rows, whole_live = (
-        lax.all_gather(data_rows, "member", axis=0, tiled=True),
+        jnp.concatenate(
+            lax.all_to_all(jnp.stack([data_rows] * lax.axis_size("member")), "member", 0, 0), axis=0
+        ),
         lax.all_gather(live_rows, "member", axis=0, tiled=True),
     )
     cost_tile = tile_cost(whole_rows, noise_rows, noise_norm, width)

time: 501 us -> 645 us (1.29)
  blocking collectives: 319 us -> 551 us
  waiting for transfers between devices: 103 us -> 16.7 us
  between operations: 13.7 us -> 0.29 us
  starting transfers between devices: 8.07 us -> 16.4 us
    all_gather x1, blocking collectives: 21.6 us -> 255 us  [body(): lax.all_gather(live_rows, 'member', axis=0, tiled=True)]
    all_gather x1 -> x0, waiting for transfers between devices: 86.4 us -> none  [body(): lax.all_gather(data_rows, 'member', axis=0, tiled=True)]
    all_to_all x0 -> x1, starting transfers between devices: none -> 8.32 us  [body(): lax.all_to_all(jnp.stack([data_rows] * lax.axis_size('member')), 'member'...]
  transfers between devices with their start and end apart: 3 -> 3, of which waited for: 3 -> 2; matrix products, arithmetic and copies ran while one was open for 2% -> 1% of each run, Pallas kernels for 0% -> 0%
where the time goes in v1:
time: 645 us; the launch traced here: 644 us
  blocking collectives  551 us (85%)
  other arithmetic  26.2 us (4%)
  matrix products  21.1 us (3%)
  waiting for transfers between devices  16.7 us (3%)
  starting transfers between devices  16.4 us (3%)
  local copies, waits for them, and re-layouts  11.9 us (2%)
    all_gather x1, blocking collectives, body(): lax.all_gather(live_rows, 'member', axis=0, tiled=True)  255 us
    psum x4, blocking collectives, body(): lax.psum(jnp.sum(jnp.exp(scores - row_peak[:, None]), axis=1), 'member')  152 us
    pmax x4, blocking collectives, body(): row_peak = lax.pmax(local_peak, 'member')  144 us
    all_to_all x1, waiting for transfers between devices, body(): lax.all_to_all(send_rows, 'bucket', split_axis=0, concat_axis=0, tiled=True)  14.5 us
  transfers between devices with their start and end apart: 3, of which 2 were waited for; matrix products, arithmetic and copies ran while one was open for 1% of the time, Pallas kernels for 0%

profile of v1, /device:TPU:2, one launch (start us, length us, event | category | flops | bytes accessed | tf_op | source)
XLA Modules:
  0.0 643.9 jit_solution(4600688152877593596)
XLA Ops:
  0.0 0.7 fusion.20
  0.7 0.1 reduce_window_sum.11
  0.8 0.8 select_reduce_fusion.7
  1.7 0.7 compare_select_fusion.1
  2.3 0.9 scatter_custom_fusion
  3.2 0.7 all_to_all.19
  3.9 4.5 all-to-all-start
  8.4 3.1 scatter_custom_fusion.2
  11.5 2.2 all-to-all-done
  13.7 3.6 all-to-all-start.1
  17.2 0.6 broadcast.142
  17.8 0.7 reduce.4
  18.5 0.1 all_to_all.21
  18.6 14.5 %all-to-all-done.1 = bf16[8,16,4096]{2,1,0:T(8,128)(2,1)S(1)} async-done(((bf16[8,16,4096]{2,1,0:T(8,128)(2,1)}), bf16[8,16,4096]{2,1,0:T(8,128)(2,1)S(1)}, u32[]{:S(2)}, u32[]{:S(2)}) %all-to-all-start.1) | async-done | bytes 1048608 | tf_op jit(solution)/shard_map/all_to_all | solution.py:34
  33.1 2.3 scatter_custom_fusion.3
  35.4 6.0 stack.2
  41.4 8.3 %all-to-all-start.2 = ((bf16[16,128,4096]{2,1,0:T(8,128)(2,1)}), bf16[16,128,4096]{2,1,0:T(8,128)(2,1)}, u32[]{:S(2)}, u32[]{:S(2)}) async-start(bf16[16,128,4096]{2,1,0:T(8,128)(2,1)} %stack.2), calls=%async_computation.2 | async-start | bytes 33554432 | tf_op jit(solution)/shard_map/all_to_all | solution.py:48
  49.7 2.5 multiply_reduce_fusion.1
  52.3 1.3 scatter_custom_fusion.1
  53.6 255.4 %all-gather = bf16[16,1,128]{2,1,0:T(2,128)(2,1)S(1)} all-gather(bf16[1,1,128]{2,1,0:T(2,128)(2,1)S(1)} %bitcast.15), channel_id=1, replica_groups=mesh['bucket'=8,'member'=16] {'member'}, dimensions={0}, use_global_device_ids=true | all-gather | bytes 4352 | tf_op jit(solution)/shard_map/all_gather | solution.py:50
  309.0 0.0 all-to-all-done.2
  309.1 0.0 copy-start
  309.1 7.5 %multiply_reduce_fusion = f32[16,128]{1,0:T(8,128)S(1)} fusion(bf16[16,128,4096]{2,1,0:T(8,128)(2,1)} %all-to-all-done.2), kind=kLoop, calls=%fused_computation.4 | loop fusion | flops 25163776 | bytes 16785408 | tf_op jit(solution)/shard_map/reduce_sum | solution.py:17
  316.6 8.5 %fusion.2 = (f32[2048]{0:T(1024)S(1)}, f32[2048,256]{1,0:T(8,128)S(1)}) fusion(bf16[2048,4096]{1,0:T(8,128)(2,1)} %bitcast.7, f32[256,4096]{1,0:T(8,128)S(1)} %copy-done, f32[256]{0:T(256)S(1)} %multiply_reduce_fusion.1, f32[2048]{0:T(1024)S(1)} %bitcast.14), kind=kOutput, calls=%fused_computation.30 | convolution fusion | flops 4299683840 | bytes 23086080 | tf_op jit(solution)/shard_map/dot_general | solution.py:12
  325.1 35.6 %pmax.28 = f32[2048]{0:T(1024)S(1)} all-reduce(f32[2048]{0:T(1024)S(1)} %get-tuple-element.5), channel_id=1, replica_groups=mesh['bucket'=8,'member'=16] {'member'}, use_global_device_ids=true, to_apply=%region_9.10 | all-reduce | flops 2048 | bytes 16384 | tf_op jit(solution)/shard_map/pmax | solution.py:60
  360.6 0.8 exponential_reduce_fusion.3
  361.4 38.4 %psum.28 = f32[2048]{0:T(1024)S(1)} all-reduce(f32[2048]{0:T(1024)S(1)} %exponential_reduce_fusion.3), channel_id=1, replica_groups=mesh['bucket'=8,'member'=16] {'member'}, use_global_device_ids=true, to_apply=%region_11.12 | all-reduce | flops 2048 | bytes 16384 | tf_op jit(solution)/shard_map/psum | solution.py:61
  399.8 0.7 select_reduce_fusion.6
  400.5 0.7 select_reduce_fusion.5
  401.3 0.3 fusion.3
  401.6 36.0 %pmax.29 = f32[2048]{0:T(1024)S(1)} all-reduce(f32[2048]{0:T(1024)S(1)} %fusion.3), channel_id=1, replica_groups=mesh['bucket'=8,'member'=16] {'member'}, use_global_device_ids=true, to_apply=%region_15.16 | all-reduce | flops 2048 | bytes 16384 | tf_op jit(solution)/shard_map/pmax | solution.py:60
  437.7 0.8 exponential_reduce_fusion.2
  438.5 38.1 %psum.29 = f32[2048]{0:T(1024)S(1)} all-reduce(f32[2048]{0:T(1024)S(1)} %exponential_reduce_fusion.2), channel_id=1, replica_groups=mesh['bucket'=8,'member'=16] {'member'}, use_global_device_ids=true, to_apply=%region_17.18 | all-reduce | flops 2048 | bytes 16384 | tf_op jit(solution)/shard_map/psum | solution.py:61
  476.6 0.7 select_reduce_fusion.4
  477.4 0.7 select_reduce_fusion.3
  478.1 0.3 fusion.4
  478.5 36.0 %pmax.30 = f32[2048]{0:T(1024)S(1)} all-reduce(f32[2048]{0:T(1024)S(1)} %fusion.4), channel_id=1, replica_groups=mesh['bucket'=8,'member'=16] {'member'}, use_global_device_ids=true, to_apply=%region_21.22 | all-reduce | flops 2048 | bytes 16384 | tf_op jit(solution)/shard_map/pmax | solution.py:60
  514.5 0.8 exponential_reduce_fusion.1
  515.3 38.0 %psum.30 = f32[2048]{0:T(1024)S(1)} all-reduce(f32[2048]{0:T(1024)S(1)} %exponential_reduce_fusion.1), channel_id=1, replica_groups=mesh['bucket'=8,'member'=16] {'member'}, use_global_device_ids=true, to_apply=%region_23.24 | all-reduce | flops 2048 | bytes 16384 | tf_op jit(solution)/shard_map/psum | solution.py:61
  553.3 0.7 select_reduce_fusion.2
  554.0 0.7 select_reduce_fusion.1
  554.7 0.3 fusion.5
  555.1 36.0 %pmax.31 = f32[2048]{0:T(1024)S(1)} all-reduce(f32[2048]{0:T(1024)S(1)} %fusion.5), channel_id=1, replica_groups=mesh['bucket'=8,'member'=16] {'member'}, use_global_device_ids=true, to_apply=%region_27.28 | all-reduce | flops 2048 | bytes 16384 | tf_op jit(solution)/shard_map/pmax | solution.py:60
  591.1 0.8 exponential_reduce_fusion
  591.9 38.0 %psum.31 = f32[2048]{0:T(1024)S(1)} all-reduce(f32[2048]{0:T(1024)S(1)} %exponential_reduce_fusion), channel_id=1, replica_groups=mesh['bucket'=8,'member'=16] {'member'}, use_global_device_ids=true, to_apply=%region_29.30 | all-reduce | flops 2048 | bytes 16384 | tf_op jit(solution)/shard_map/psum | solution.py:61
  629.9 0.7 select_reduce_fusion
  630.6 0.7 fusion.6
  631.3 12.6 %fusion.7 = f32[256,4096]{1,0:T(8,128)} fusion(bf16[2048,4096]{1,0:T(8,128)(2,1)} %bitcast.7, f32[2048,256]{1,0:T(8,128)S(1)} %get-tuple-element.6, f32[256]{0:T(256)S(1)} %fusion.6, f32[256]{0:T(256)S(1)} %select_reduce_fusion, f32[2048]{0:T(1024)S(1)} %add_multiply_fusion, pred[2048]{0:T(1024)(128)(4,1)S(1)} %compare_bitcast_fusion), kind=kOutput, calls=%fused_computation.35 | convolution fusion | flops 4298113024 | bytes 23080960 | tf_op jit(solution)/shard_map/dot_general | solution.py:69
  (11 shorter events, 0.1 us)
Async XLA Ops:
  3.9 9.7 %all-to-all-start = ((s32[8,16,1]{1,2,0:T(1,128)}), s32[8,16,1]{1,2,0:T(1,128)S(1)}, u32[]{:S(2)}, u32[]{:S(2)}) async-start(s32[8,16,1]{1,2,0:T(1,128)} %bitcast), calls=%async_computation | async-start | bytes 8192 | tf_op jit(solution)/shard_map/all_to_all | solution.py:35
  13.7 19.5 %all-to-all-start.1 = ((bf16[8,16,4096]{2,1,0:T(8,128)(2,1)}), bf16[8,16,4096]{2,1,0:T(8,128)(2,1)S(1)}, u32[]{:S(2)}, u32[]{:S(2)}) async-start(bf16[8,16,4096]{2,1,0:T(8,128)(2,1)} %bitcast.4), calls=%async_computation.1 | async-start | bytes 2097152 | tf_op jit(solution)/shard_map/all_to_all | solution.py:34
  41.4 267.7 %all-to-all-start.2 = ((bf16[16,128,4096]{2,1,0:T(8,128)(2,1)}), bf16[16,128,4096]{2,1,0:T(8,128)(2,1)}, u32[]{:S(2)}, u32[]{:S(2)}) async-start(bf16[16,128,4096]{2,1,0:T(8,128)(2,1)} %stack.2), calls=%async_computation.2 | async-start | bytes 33554432 | tf_op jit(solution)/shard_map/all_to_all | solution.py:48
  309.1 7.5 %copy-start = (f32[256,4096]{1,0:T(8,128)S(1)}, f32[256,4096]{1,0:T(8,128)}, u32[]{:S(2)}) copy-start(f32[256,4096]{1,0:T(8,128)} %param.7) | copy-start | bytes 12582916
